TPU v7x, 32 devices: a whole 2x2x4 slice. The times are simulated.
32 devices in a mesh: groups: 2 (over x), gx: 16 (over z, y, core).
Axes of the slice: x: 2, y: 2, z: 4, core: 2. Of those that a mesh axis runs over, the one named last changes fastest.
Arguments:
- velocity: bfloat16 [3, 16, 128, 128], P(None, 'groups', 'gx'), parts along dimension 1, may hold values from -5 to 5
- offsets: int32 [6], P('groups'), parts along dimension 0, may hold values from 0 to 1023
- conv_in: bfloat16 [64, 9, 3, 3], replicated, may hold values from -0.625 to 0.625
- conv_mid: bfloat16 [64, 64, 3, 3], replicated, may hold values from -0.25 to 0.25
- conv_out: bfloat16 [36, 64, 3, 3], replicated, may hold values from -0.25 to 0.25
- cotangent: float32 [3, 8, 128, 128], P(None, 'groups', 'gx'), parts along dimension 1, may hold values from -6 to 6
Outputs:
- final_state: float32 [3, 8, 128, 128], P(None, 'groups', 'gx'), parts along dimension 1
- weight_grads: bfloat16 [36, 8, 128, 128], P(None, 'groups', 'gx'), parts along dimension 1
There are 2 independent parts, one for each index of `groups`. A program takes and returns all parts, laid end to end along the dimension named above; an argument that names none is the same for every part. Nothing has to cross between parts.
All inputs are finite; a program needn't handle non-finite values.
Results may differ from a plain program's by a relative error of at most 0.0045.
Values may be sent and summed in bfloat16 or wider, within the bound.
No kernel may reach another device: no remote copies, remote signals or barrier semaphores. Data moves between devices by JAX's collectives and lax.ppermute only.
A program may use at most 128 MiB of HBM per device.

v0:
```python
import math
import jax
import jax.numpy as jnp
from jax import lax
from jax.sharding import PartitionSpec as P

DOMAIN = 1024
SPREAD = 0.25
STEP_SIZE = 0.3
BASE_TAPS = (-0.0625, 0.5625, 0.5625, -0.0625)


def with_halo(shard, sides, width):
    for axis, dim in sides:
        size, length = (lax.axis_size(axis), shard.shape[dim])
        up = [(i, (i + 1) % size) for i in range(size)]
        down = [(j, i) for i, j in up]
        last = lax.slice_in_dim(shard, length - width, length, axis=dim)
        leading = lax.slice_in_dim(shard, 0, width, axis=dim)
        before = lax.ppermute(last, axis, up)
        after = lax.ppermute(leading, axis, down)
        shard = jnp.concatenate([before, shard, after], axis=dim)
    return shard


def shortened(shard):

    def short(part):
        return part.astype(jnp.bfloat16) if part.dtype == jnp.float32 else part

    return jax.tree.map(short, shard)


def phase_angle(coords, offset):
    return (coords + offset).astype(jnp.float32) * (2.0 * math.pi / DOMAIN)


def positions(zcoord, ycoord, xcoord, offsets):
    angle_z = phase_angle(zcoord, offsets[2])[:, None, None]
    angle_y = phase_angle(ycoord, offsets[1])
    angle_x = phase_angle(xcoord, offsets[0])
    angle_y = angle_y[None, :, None]
    angle_x = angle_x[None, None, :]
    zero_grid = jnp.zeros_like(angle_z + angle_y + angle_x)
    channel_list = [
        jnp.sin(angle_x),
        jnp.cos(angle_x),
        jnp.sin(angle_y),
        jnp.cos(angle_y),
        jnp.sin(angle_z),
        jnp.cos(angle_z),
    ]
    return jnp.stack([item + zero_grid for item in channel_list], axis=0)


def wrap_pad(values, margin, axis_list):
    for roll_axis in axis_list:
        extent = values.shape[roll_axis]
        values = jnp.concatenate(
            [
                lax.slice_in_dim(values, extent - margin, extent, axis=roll_axis),
                values,
                lax.slice_in_dim(values, 0, margin, axis=roll_axis),
            ],
            axis=roll_axis,
        )
    return values


def conv_layer(inputs, kernel, kernel_layout):
    return lax.conv_general_dilated(
        inputs,
        kernel,
        (1, 1),
        "VALID",
        dimension_numbers=("CNHW", kernel_layout, "CNHW"),
        preferred_element_type=jnp.float32,
    )


def interpolation(raw_output):
    grouped = raw_output.reshape((3, 3, 4) + raw_output.shape[1:])
    base_taps = jnp.array(BASE_TAPS, dtype=jnp.float32).reshape(
        (1, 1, 4) + (1,) * (raw_output.ndim - 1)
    )
    mixed = base_taps + SPREAD * (grouped - jnp.mean(grouped, axis=2, keepdims=True))
    return mixed.reshape(raw_output.shape).astype(jnp.bfloat16)


def network(inputs, conv_in, conv_mid, conv_out, kernel_layout):
    first = jax.nn.gelu(conv_layer(inputs, conv_in, kernel_layout)).astype(jnp.bfloat16)
    second = jax.nn.gelu(conv_layer(first, conv_mid, kernel_layout)).astype(jnp.bfloat16)
    return interpolation(conv_layer(second, conv_out, kernel_layout))


def advect(padded, weights, row_direction):
    rows = padded.shape[2] - 4
    depth = padded.shape[1] - 4
    middle = padded[:, 2 : 2 + depth, 2 : 2 + rows]
    grouped = weights.reshape((3, 3, 4) + middle.shape[1:])
    change = jnp.zeros_like(middle)
    for direction in (0, 1, 2):
        nearby = {}
        for offset in (-2, -1, 0, 1, 2):
            if direction == 2:
                nearby[offset] = padded[:, 2 + offset : 2 + offset + depth, 2 : 2 + rows]
            elif direction == row_direction:
                nearby[offset] = padded[:, 2 : 2 + depth, 2 + offset : 2 + offset + rows]
            else:
                nearby[offset] = jnp.roll(middle, -offset, axis=3)
        speed_up = 0.5 * (middle[direction] + nearby[1][direction])
        speed_down = 0.5 * (middle[direction] + nearby[-1][direction])
        face_up = sum(
            (grouped[:, direction, tap_index] * nearby[tap_index - 1] for tap_index in range(4))
        )
        face_down = sum(
            (grouped[:, direction, tap_index] * nearby[tap_index - 2] for tap_index in range(4))
        )
        change = change + speed_up * face_up - speed_down * face_down
    return middle - STEP_SIZE * change


def halo_rows(values):
    return with_halo(values, (("gx", 2),), 2)


def on_device(velocity, offsets, conv_in, conv_mid, conv_out, cotangent):
    depth = velocity.shape[1] - 4
    row_count = velocity.shape[2]
    devices = lax.axis_size("gx")
    position = lax.axis_index("gx")
    total_cells = row_count * devices
    zcoord = jnp.arange(depth, dtype=jnp.int32)
    extended = with_halo(velocity[:, 2 : 2 + depth], (("gx", 2),), 3)
    ycoord = (position * row_count - 3 + jnp.arange(row_count + 6, dtype=jnp.int32)) % total_cells
    xcoord = (jnp.arange(total_cells + 6, dtype=jnp.int32) - 3) % total_cells
    features = positions(zcoord, ycoord, xcoord, offsets).astype(jnp.bfloat16)
    inputs = jnp.concatenate([wrap_pad(extended, 3, (3,)), features], axis=0)
    stencil = network(inputs, conv_in, conv_mid, conv_out, "OIHW")
    row_direction = 1
    block_cotangent = jnp.swapaxes(
        lax.all_to_all(cotangent, "gx", split_axis=3, concat_axis=2, tiled=True), 2, 3
    )
    weights = stencil.astype(jnp.float32)
    start = velocity.astype(jnp.float32)
    ghost_low = start[:, :2]
    ghost_high = start[:, 2 + depth :]

    def step(padded, weight_values):
        return advect(padded, weight_values, row_direction)

    padded_start = halo_rows(start)
    middle, pull_first = jax.vjp(step, padded_start, weights)
    padded_middle = halo_rows(jnp.concatenate([ghost_low, middle, ghost_high], axis=1))
    block_final, pull_second = jax.vjp(step, padded_middle, weights)
    back_padded, grad_second = pull_second(block_cotangent)
    back_inner = back_padded[:, 2 : 2 + depth]
    rim_rows = jnp.concatenate([back_inner[:, :, :2], back_inner[:, :, -2:]], axis=2)
    beside_all = with_halo(shortened(rim_rows), (("gx", 2),), 2).astype(rim_rows.dtype)
    middle_grad = jnp.concatenate(
        [
            back_inner[:, :, 2:4] + beside_all[:, :, :2],
            back_inner[:, :, 4:-4],
            back_inner[:, :, -4:-2] + beside_all[:, :, -2:],
        ],
        axis=2,
    )
    unused_grad, grad_first = pull_first(middle_grad)
    weight_grads = (grad_first + grad_second).astype(jnp.bfloat16)
    final_state = jnp.swapaxes(
        lax.all_to_all(block_final, "gx", split_axis=3, concat_axis=2, tiled=True), 2, 3
    )
    return (final_state, weight_grads)


def solution(mesh):
    return jax.shard_map(
        on_device,
        mesh=mesh,
        in_specs=(
            P(None, "groups", "gx", None),
            P("groups"),
            P(),
            P(),
            P(),
            P(None, "groups", "gx", None),
        ),
        out_specs=(P(None, "groups", "gx", None), P(None, "groups", "gx", None)),
        check_vma=False,
    )
```

profile of v0, /device:TPU:0, one launch (start us, length us, event | category | flops | bytes accessed | tf_op | source)
XLA Modules:
  0.0 85.5 jit_solution(15485054560610476140)
XLA Ops:
  2.0 5.1 %collective-permute-start.1 = (bf16[3,4,3,128]{3,2,1,0:T(4,128)(2,1)S(1)}, bf16[3,4,3,128]{3,2,1,0:T(4,128)(2,1)S(1)}, u32[]{:S(2)}, u32[]{:S(2)}) collective-permute-start(bf16[3,4,3,128]{3,2,1,0:T(4,128)(2,1)S(1)} %get-tuple-element.171), channel_id=1, source_target_pairs={{1,0},{2,1},{3,2},{4,3},{5,4},{6,5},{7,6},{8,7},{9,8},{10,9},{11,1... | collective-permute-start | bytes 27656 | tf_op jit(solution)/shard_map/ppermute | solution.py:21
  7.1 1.5 %fusion.141 = (f32[3,8,2,128]{3,2,1,0:T(2,128)}, f32[3,8,2,128]{3,2,1,0:T(2,128)}) fusion(bf16[3,8,8,128]{3,2,1,0:T(8,128)(2,1)} %param.7), kind=kLoop, calls=%fused_computation.326 | loop fusion | bytes 98304 | tf_op jit(solution)/shard_map/slice | solution.py:19
  9.3 1.1 %copy.106 = f32[3,4,8,128]{2,1,0,3:T(4,128)S(1)} copy(f32[3,4,8,128]{3,2,1,0:T(8,128)} %param.12) | data formatting | bytes 98304 | tf_op args[5]
  10.4 1.4 %reshape.458 = f32[16,1,768]{2,1,0:T(1,128)} reshape(f32[128,3,4,8]{3,2,1,0:T(4,128)S(1)} %bitcast.472) | data formatting | bytes 98304
  11.8 5.9 %all-to-all-start.1 = ((f32[16,1,768]{2,1,0:T(1,128)}), f32[16,1,768]{2,1,0:T(1,128)}, u32[]{:S(2)}, u32[]{:S(2)}) async-start(f32[16,1,768]{2,1,0:T(1,128)} %reshape.458), calls=%async_computation.1 | async-start | bytes 98304 | tf_op jit(solution)/shard_map/all_to_all | solution.py:142
  18.5 1.5 %fusion.144 = (f32[3,4,8,1]{3,2,1,0:T(8,128)}, f32[3,4,8,1]{3,2,1,0:T(8,128)S(1)}) fusion(bf16[3,8,8,128]{3,2,1,0:T(8,128)(2,1)} %param.7), kind=kLoop, calls=%fused_computation.329 | loop fusion | bytes 1536 | tf_op jit(solution)/shard_map/jvp(jit(_roll_static))/slice | solution.py:110
  30.4 1.9 %copy.88 = bf16[9,14,32,19]{2,0,3,1:T(8,128)(2,1)S(1)} copy(bf16[9,14,32,19]{3,2,1,0:T(8,128)(2,1)S(1)} %fusion.36) | data formatting | bytes 306432 | tf_op jit(solution)/shard_map/conv_general_dilated | solution.py:71
  32.3 4.4 %select_bitcast_fusion = bf16[12,4,8,17,64]{4,2,1,3,0:T(8,128)(2,1)S(1)} fusion(pred[32,17]{0,1:T(8,128)(4,1)S(1)} %copy-done.23, bf16[9,14,32,19]{2,0,3,1:T(8,128)(2,1)S(1)} %copy.88, bf16[64,9,3,3]{0,3,2,1:T(4,128)(2,1)} %param.9), kind=kOutput, calls=%fused_computation.30 | convolution fusion | flops 72278016 | bytes 999712 | tf_op jit(solution)/shard_map/conv_general_dilated | solution.py:71
  36.9 4.0 %select_bitcast_fusion.1 = bf16[10,4,8,17,64]{4,2,1,3,0:T(8,128)(2,1)S(1)} fusion(pred[32,17]{0,1:T(8,128)(4,1)S(1)} %copy-done.22, bf16[64,64,3,3]{1,0,3,2:T(8,128)(2,1)S(1)} %copy-done, bf16[12,4,7,2,64]{4,2,1,3,0:T(8,128)(2,1)S(1)} %slice.444, bf16[12,4,8,17,64]{4,2,1,3,0:T(8,128)(2,1)S(1)} %select_bitcast_fusion), kind=kOutput, calls=%fused_computation.37 | convolution fusion | flops 407363584 | bytes 1692192 | tf_op jit(solution)/shard_map/conv_general_dilated | solution.py:71
  40.9 2.9 %fusion.28 = f32[8,32,17,36]{3,1,2,0:T(8,128)S(1)} fusion(bf16[36,64,3,3]{1,0,3,2:T(8,128)(2,1)S(1)} %copy-done.21, bf16[10,4,7,2,64]{4,2,1,3,0:T(8,128)(2,1)S(1)} %slice.445, bf16[10,4,8,17,64]{4,2,1,3,0:T(8,128)(2,1)S(1)} %select_bitcast_fusion.1), kind=kOutput, calls=%fused_computation.33 | convolution fusion | flops 182820864 | bytes 1436160 | tf_op jit(solution)/shard_map/conv_general_dilated | solution.py:71
  43.8 1.3 %copy.90 = f32[8,32,17,36]{3,0,2,1:T(8,128)S(1)} copy(f32[8,32,17,36]{3,1,2,0:T(8,128)S(1)} %fusion.28) | data formatting | bytes 1253376 | tf_op jit(solution)/shard_map/conv_general_dilated | solution.py:71
  46.9 1.3 %broadcast_multiply_fusion.1 = (f32[4,8,128]{2,1,0:T(8,128)S(1)}, f32[4,8,128]{2,1,0:T(8,128)S(1)}, f32[4,8,128]{2,1,0:T(8,128)S(1)}, f32[4,8,128]{2,1,0:T(8,128...) fusion(f32[3,4,8,1]{3,2,1,0:T(8,128)S(1)} %get-tuple-element.173, f32[3,4,8,127]{3,2,1,0:T(8,128)S(1)} %get-tuple-element.175, ...), kind=kLoop, calls=%fused_computation.273 | loop fusion | flops 45056 | bytes 385024 | tf_op jit(solution)/shard_map/transpose(jvp())/mul | solution.py:119
  49.0 1.0 %fusion.57 = f32[3,4,8,128]{3,2,1,0:T(8,128)S(1)} fusion(f32[3,4,8,2]{3,2,1,0:T(8,128)S(1)} %copy-done.5, f32[3,4,8,126]{3,2,1,0:T(8,128)S(1)} %copy-done.7, f32[3,4,8,126]{3,2,1,0:T(8,128)S(1)} %copy-done.6, f32[3,4,8,2]{3,2,1,0:T(8,128)S(1)} %copy-done.4, f32[3,8,8,128]{3,2,1,0:T(8,128)S(1)} %convert_element_type.54, ...), kind=kLoop, calls=%fused_computation.113 | loop fusion | flops 774144 | bytes 1523712 | tf_op jit(solution)/shard_map/jvp()/sub | solution.py:120
  50.2 4.4 %collective-permute-start.4 = (f32[3,8,2,128]{3,2,1,0:T(2,128)S(1)}, f32[3,8,2,128]{3,2,1,0:T(2,128)S(1)}, u32[]{:S(2)}, u32[]{:S(2)}) collective-permute-start(f32[3,8,2,128]{3,2,1,0:T(2,128)S(1)} %get-tuple-element.111), channel_id=1, source_target_pairs={{1,0},{2,1},{3,2},{4,3},{5,4},{6,5},{7,6},{8,7},{9,8},{10,9},{11,1... | collective-permute-start | bytes 73736 | tf_op jit(solution)/shard_map/ppermute | solution.py:21
  54.7 1.4 %collective-permute-done.4 = f32[3,8,2,128]{3,2,1,0:T(2,128)S(1)} collective-permute-done((f32[3,8,2,128]{3,2,1,0:T(2,128)S(1)}, f32[3,8,2,128]{3,2,1,0:T(2,128)S(1)}, u32[]{:S(2)}, u32[]{:S(2)}) %collective-permute-start.4) | collective-permute-done | bytes 24608 | tf_op jit(solution)/shard_map/ppermute | solution.py:21
  56.2 4.4 %collective-permute-done.5 = f32[3,8,2,128]{3,2,1,0:T(2,128)S(1)} collective-permute-done((f32[3,8,2,128]{3,2,1,0:T(2,128)S(1)}, f32[3,8,2,128]{3,2,1,0:T(2,128)S(1)}, u32[]{:S(2)}, u32[]{:S(2)}) %collective-permute-start.5) | collective-permute-done | bytes 24608 | tf_op jit(solution)/shard_map/ppermute | solution.py:20
  61.2 1.5 %reduce = f32[16,768]{1,0:T(8,128)S(1)} reduce(f32[16,1,768]{2,1,0:T(1,128)} %all-to-all-done.1, f32[]{:T(128)} %broadcast.630), dimensions={1}, to_apply=%all_to_all.30.reduce_sub_computation | reduce | bytes 98308 | tf_op jit(solution)/shard_map/all_to_all | solution.py:142
  62.8 0.9 %reshape.459 = f32[128,3,4,8]{3,2,1,0:T(4,128)S(1)} reshape(f32[16,768]{1,0:T(8,128)S(1)} %reduce) | data formatting | bytes 98304
  65.8 4.4 %collective-permute-start.7 = (bf16[3,4,2,128]{3,2,1,0:T(2,128)(2,1)S(1)}, bf16[3,4,2,128]{3,2,1,0:T(2,128)(2,1)}, u32[]{:S(2)}, u32[]{:S(2)}) collective-permute-start(bf16[3,4,2,128]{3,2,1,0:T(2,128)(2,1)S(1)} %get-tuple-element.95), channel_id=1, source_target_pairs={{1,0},{2,1},{3,2},{4,3},{5,4},{6,5},{7,6},{8,7},{9,8},{10,9},{11,1... | collective-permute-start | bytes 18440 | tf_op jit(solution)/shard_map/ppermute | solution.py:21
  70.7 1.4 %reshape.456 = f32[16,1,768]{2,1,0:T(1,128)} reshape(f32[128,3,4,8]{3,2,1,0:T(4,128)S(1)} %bitcast.469) | data formatting | bytes 98304
  72.1 3.5 %all-to-all-start = ((f32[16,1,768]{2,1,0:T(1,128)}), f32[16,1,768]{2,1,0:T(1,128)S(1)}, u32[]{:S(2)}, u32[]{:S(2)}) async-start(f32[16,1,768]{2,1,0:T(1,128)} %reshape.456), calls=%async_computation | async-start | bytes 98304 | tf_op jit(solution)/shard_map/all_to_all | solution.py:171
  80.0 2.4 %all-to-all-done = f32[16,1,768]{2,1,0:T(1,128)S(1)} async-done(((f32[16,1,768]{2,1,0:T(1,128)}), f32[16,1,768]{2,1,0:T(1,128)S(1)}, u32[]{:S(2)}, u32[]{:S(2)}) %all-to-all-start) | async-done | bytes 49184 | tf_op jit(solution)/shard_map/all_to_all | solution.py:171
  83.1 0.9 %reshape.457 = f32[128,3,4,8]{3,2,1,0:T(4,128)S(1)} reshape(f32[16,768]{1,0:T(8,128)S(1)} %reduce.1) | data formatting | bytes 98304
  84.5 0.9 %all_to_all.29 = f32[3,4,128,8]{2,3,1,0:T(8,128)} reshape(f32[3,4,16,8,8]{3,2,4,1,0:T(8,128)S(1)} %bitcast.471) | data formatting | bytes 98304 | tf_op jit(solution)/shard_map/all_to_all | solution.py:171
  (144 shorter events, 24.5 us)
Async XLA Ops:
  0.6 36.2 %copy-start = (bf16[64,64,3,3]{1,0,3,2:T(8,128)(2,1)S(1)}, bf16[64,64,3,3]{1,0,3,2:T(8,128)(2,1)}, u32[]{:S(2)}) copy-start(bf16[64,64,3,3]{1,0,3,2:T(8,128)(2,1)} %param.10) | copy-start | bytes 221188
  0.6 27.0 %copy-start.20 = (f32[4]{0:T(128)S(1)}, f32[4]{0:T(128)}, u32[]{:S(2)}) copy-start(f32[4]{0:T(128)} %constant.69.clone) | copy-start | bytes 52
  0.7 19.4 %copy-start.1 = (bf16[3,8,8,128]{3,2,1,0:T(8,128)(2,1)S(1)}, bf16[3,8,8,128]{3,2,1,0:T(8,128)(2,1)}, u32[]{:S(2)}) copy-start(bf16[3,8,8,128]{3,2,1,0:T(8,128)(2,1)} %param.7) | copy-start | bytes 147460
  0.7 24.2 %copy-start.19 = (s32[3]{0:T(128)S(1)}, s32[3]{0:T(128)}, u32[]{:S(2)}) copy-start(s32[3]{0:T(128)} %param.8) | copy-start | bytes 40
  1.5 26.2 %collective-permute-start = (bf16[3,4,3,128]{3,2,1,0:T(4,128)(2,1)S(1)}, bf16[3,4,3,128]{3,2,1,0:T(4,128)(2,1)S(1)}, u32[]{:S(2)}, u32[]{:S(2)}) collective-permute-start(bf16[3,4,3,128]{3,2,1,0:T(4,128)(2,1)S(1)} %get-tuple-element.170), channel_id=1, source_target_pairs={{0,1},{1,2},{2,3},{3,4},{4,5},{5,6},{6,7},{7,8},{8,9},{9,10},{10,1... | collective-permute-start | bytes 27656 | tf_op jit(solution)/shard_map/ppermute | solution.py:20
  2.0 25.7 %collective-permute-start.1 = (bf16[3,4,3,128]{3,2,1,0:T(4,128)(2,1)S(1)}, bf16[3,4,3,128]{3,2,1,0:T(4,128)(2,1)S(1)}, u32[]{:S(2)}, u32[]{:S(2)}) collective-permute-start(bf16[3,4,3,128]{3,2,1,0:T(4,128)(2,1)S(1)} %get-tuple-element.171), channel_id=1, source_target_pairs={{1,0},{2,1},{3,2},{4,3},{5,4},{6,5},{7,6},{8,7},{9,8},{10,9},{11,1... | collective-permute-start | bytes 27656 | tf_op jit(solution)/shard_map/ppermute | solution.py:21
  8.6 38.3 %collective-permute-start.2 = (f32[3,8,2,128]{3,2,1,0:T(2,128)}, f32[3,8,2,128]{3,2,1,0:T(2,128)}, u32[]{:S(2)}, u32[]{:S(2)}) collective-permute-start(f32[3,8,2,128]{3,2,1,0:T(2,128)} %get-tuple-element.166), channel_id=1, source_target_pairs={{1,0},{2,1},{3,2},{4,3},{5,4},{6,5},{7,6},{8,7},{9,8},{10,9},{11,1... | collective-permute-start | bytes 73736 | tf_op jit(solution)/shard_map/ppermute | solution.py:21
  9.3 38.9 %collective-permute-start.3 = (f32[3,8,2,128]{3,2,1,0:T(2,128)}, f32[3,8,2,128]{3,2,1,0:T(2,128)}, u32[]{:S(2)}, u32[]{:S(2)}) collective-permute-start(f32[3,8,2,128]{3,2,1,0:T(2,128)} %get-tuple-element.167), channel_id=1, source_target_pairs={{0,1},{1,2},{2,3},{3,4},{4,5},{5,6},{6,7},{7,8},{8,9},{9,10},{10,1... | collective-permute-start | bytes 73736 | tf_op jit(solution)/shard_map/ppermute | solution.py:20
  11.8 48.9 %all-to-all-start.1 = ((f32[16,1,768]{2,1,0:T(1,128)}), f32[16,1,768]{2,1,0:T(1,128)}, u32[]{:S(2)}, u32[]{:S(2)}) async-start(f32[16,1,768]{2,1,0:T(1,128)} %reshape.458), calls=%async_computation.1 | async-start | bytes 98304 | tf_op jit(solution)/shard_map/all_to_all | solution.py:142
  48.9 7.2 %copy-start.16 = (f32[4,8,128]{2,1,0:T(8,128)}, f32[4,8,128]{2,1,0:T(8,128)S(1)}, u32[]{:S(2)}) copy-start(f32[4,8,128]{2,1,0:T(8,128)S(1)} %get-tuple-element.117) | copy-start | bytes 49156
  50.2 5.9 %collective-permute-start.4 = (f32[3,8,2,128]{3,2,1,0:T(2,128)S(1)}, f32[3,8,2,128]{3,2,1,0:T(2,128)S(1)}, u32[]{:S(2)}, u32[]{:S(2)}) collective-permute-start(f32[3,8,2,128]{3,2,1,0:T(2,128)S(1)} %get-tuple-element.111), channel_id=1, source_target_pairs={{1,0},{2,1},{3,2},{4,3},{5,4},{6,5},{7,6},{8,7},{9,8},{10,9},{11,1... | collective-permute-start | bytes 73736 | tf_op jit(solution)/shard_map/ppermute | solution.py:21
  54.7 6.0 %collective-permute-start.5 = (f32[3,8,2,128]{3,2,1,0:T(2,128)S(1)}, f32[3,8,2,128]{3,2,1,0:T(2,128)S(1)}, u32[]{:S(2)}, u32[]{:S(2)}) collective-permute-start(f32[3,8,2,128]{3,2,1,0:T(2,128)S(1)} %get-tuple-element.110), channel_id=1, source_target_pairs={{0,1},{1,2},{2,3},{3,4},{4,5},{5,6},{6,7},{7,8},{8,9},{9,10},{10,1... | collective-permute-start | bytes 73736 | tf_op jit(solution)/shard_map/ppermute | solution.py:20
  65.6 11.0 %copy-start.17 = (f32[4,8,128]{2,1,0:T(8,128)S(1)}, f32[4,8,128]{2,1,0:T(8,128)}, u32[]{:S(2)}) copy-start(f32[4,8,128]{2,1,0:T(8,128)} %copy-done.16) | copy-start | bytes 49156
  65.6 11.1 %copy-start.18 = (f32[4,8,128]{2,1,0:T(8,128)S(1)}, f32[4,8,128]{2,1,0:T(8,128)}, u32[]{:S(2)}) copy-start(f32[4,8,128]{2,1,0:T(8,128)} %get-tuple-element.114) | copy-start | bytes 49156
  65.7 10.0 %collective-permute-start.6 = (bf16[3,4,2,128]{3,2,1,0:T(2,128)(2,1)S(1)}, bf16[3,4,2,128]{3,2,1,0:T(2,128)(2,1)}, u32[]{:S(2)}, u32[]{:S(2)}) collective-permute-start(bf16[3,4,2,128]{3,2,1,0:T(2,128)(2,1)S(1)} %get-tuple-element.94), channel_id=1, source_target_pairs={{0,1},{1,2},{2,3},{3,4},{4,5},{5,6},{6,7},{7,8},{8,9},{9,10},{10,1... | collective-permute-start | bytes 18440 | tf_op jit(solution)/shard_map/ppermute | solution.py:20
  65.8 9.9 %collective-permute-start.7 = (bf16[3,4,2,128]{3,2,1,0:T(2,128)(2,1)S(1)}, bf16[3,4,2,128]{3,2,1,0:T(2,128)(2,1)}, u32[]{:S(2)}, u32[]{:S(2)}) collective-permute-start(bf16[3,4,2,128]{3,2,1,0:T(2,128)(2,1)S(1)} %get-tuple-element.95), channel_id=1, source_target_pairs={{1,0},{2,1},{3,2},{4,3},{5,4},{6,5},{7,6},{8,7},{9,8},{10,9},{11,1... | collective-permute-start | bytes 18440 | tf_op jit(solution)/shard_map/ppermute | solution.py:21
  70.3 6.5 %copy-start.12 = (f32[3,1,1,4,8,2]{5,4,3,0,2,1:T(8,128)S(1)}, f32[3,1,1,4,8,2]{5,4,3,0,2,1:T(8,128)}, u32[]{:S(2)}) copy-start(f32[3,1,1,4,8,2]{5,4,3,0,2,1:T(8,128)} %get-tuple-element.86) | copy-start | bytes 2308
  70.3 6.5 %copy-start.13 = (f32[3,1,1,4,8,126]{5,4,3,0,2,1:T(8,128)S(1)}, f32[3,1,1,4,8,126]{5,4,3,0,2,1:T(8,128)}, u32[]{:S(2)}) copy-start(f32[3,1,1,4,8,126]{5,4,3,0,2,1:T(8,128)} %get-tuple-element.88) | copy-start | bytes 145156
  70.3 6.5 %copy-start.14 = (f32[3,1,1,4,8,127]{5,4,3,0,2,1:T(8,128)S(1)}, f32[3,1,1,4,8,127]{5,4,3,0,2,1:T(8,128)}, u32[]{:S(2)}) copy-start(f32[3,1,1,4,8,127]{5,4,3,0,2,1:T(8,128)} %get-tuple-element.90) | copy-start | bytes 146308
  70.3 6.6 %copy-start.8 = (f32[3,1,1,4,8,2]{5,4,3,0,2,1:T(8,128)S(1)}, f32[3,1,1,4,8,2]{5,4,3,0,2,1:T(8,128)}, u32[]{:S(2)}) copy-start(f32[3,1,1,4,8,2]{5,4,3,0,2,1:T(8,128)} %get-tuple-element.87) | copy-start | bytes 2308
  70.3 6.6 %copy-start.9 = (f32[3,1,1,4,8,126]{5,4,3,0,2,1:T(8,128)S(1)}, f32[3,1,1,4,8,126]{5,4,3,0,2,1:T(8,128)}, u32[]{:S(2)}) copy-start(f32[3,1,1,4,8,126]{5,4,3,0,2,1:T(8,128)} %get-tuple-element.89) | copy-start | bytes 145156
  70.3 6.6 %copy-start.10 = (f32[3,1,1,4,8,127]{5,4,3,0,2,1:T(8,128)S(1)}, f32[3,1,1,4,8,127]{5,4,3,0,2,1:T(8,128)}, u32[]{:S(2)}) copy-start(f32[3,1,1,4,8,127]{5,4,3,0,2,1:T(8,128)} %get-tuple-element.91) | copy-start | bytes 146308
  70.3 6.6 %copy-start.11 = (f32[3,1,1,4,8,1]{5,4,3,0,2,1:T(8,128)S(1)}, f32[3,1,1,4,8,1]{5,4,3,0,2,1:T(8,128)}, u32[]{:S(2)}) copy-start(f32[3,1,1,4,8,1]{5,4,3,0,2,1:T(8,128)} %get-tuple-element.93) | copy-start | bytes 1156
  72.1 10.2 %all-to-all-start = ((f32[16,1,768]{2,1,0:T(1,128)}), f32[16,1,768]{2,1,0:T(1,128)S(1)}, u32[]{:S(2)}, u32[]{:S(2)}) async-start(f32[16,1,768]{2,1,0:T(1,128)} %reshape.456), calls=%async_computation | async-start | bytes 98304 | tf_op jit(solution)/shard_map/all_to_all | solution.py:171
  (10 other events, 32.9 us)
where the time goes:
time: 86.4 us; the launch traced here: 85.5 us
  local copies, waits for them, and re-layouts  26.2 us (30%)
  starting transfers between devices  24.5 us (28%)
  other arithmetic  13.9 us (16%)
  matrix products  11.3 us (13%)
  waiting for transfers between devices  8.24 us (10%)
  between operations  1.44 us (2%)
    ppermute x4, starting transfers between devices, with_halo(): after = lax.ppermute(leading, axis, down)  14.5 us
    conv_general_dilated x3, matrix products, conv_layer(): lax.conv_general_dilated(inputs, kernel, (1, 1), 'VALID', dimension_numbe...  11.3 us
    unnamed x60, local copies, waits for them, and re-layouts  7.5 us
    all_to_all x1, starting transfers between devices, on_device(): lax.all_to_all(cotangent, 'gx', split_axis=3, concat_axis=2, tiled=True)  5.86 us
    ppermute x4, waiting for transfers between devices, with_halo(): before = lax.ppermute(last, axis, up)  4.43 us
    conv_general_dilated x5, local copies, waits for them, and re-layouts, conv_layer(): lax.conv_general_dilated(inputs, kernel, (1, 1), 'VALID', dimension_numbe...  4.36 us
    slice x8, local copies, waits for them, and re-layouts, advect(): nearby[offset] = jnp.roll(middle, -offset, axis=3)  3.83 us
    all_to_all x1, starting transfers between devices, on_device(): lax.all_to_all(block_final, 'gx', split_axis=3, concat_axis=2, tiled=True)  3.5 us
  transfers between devices with their start and end apart: 10, of which 3 were waited for; matrix products, arithmetic and copies ran while one was open for 49% of the time, Pallas kernels for 0%

commit v1 on v0

--- a/solution.py
+++ b/solution.py
@@ -168,7 +168,14 @@
     unused_grad, grad_first = pull_first(middle_grad)
     weight_grads = (grad_first + grad_second).astype(jnp.bfloat16)
     final_state = jnp.swapaxes(
-        lax.all_to_all(block_final, "gx", split_axis=3, concat_axis=2, tiled=True), 2, 3
+        jnp.concatenate(
+            lax.all_to_all(
+                jnp.stack(jnp.split(block_final, lax.axis_size("gx"), axis=3)), "gx", 0, 0
+            ),
+            axis=2,
+        ),
+        2,
+        3,
     )
     return (final_state, weight_grads)
 

time: 86.4 us -> 86.3 us (level)
    all_to_all x2 -> x0, local copies, waits for them, and re-layouts: 1.41 us -> none  [on_device(): lax.all_to_all(block_final, 'gx', split_axis=3, concat_axis=2, tiled=True)]
    reshape x0 -> x2, local copies, waits for them, and re-layouts: none -> 1.34 us  [on_device(): jnp.concatenate(lax.all_to_all(jnp.stack(jnp.split(block_final, lax.axis_...]
    unnamed x60 -> x75, local copies, waits for them, and re-layouts: 7.5 us -> 7.73 us
  transfers between devices with their start and end apart: 10 -> 10, of which waited for: 3 -> 3; matrix products, arithmetic and copies ran while one was open for 49% -> 50% of each run, Pallas kernels for 0% -> 0%
where the time goes in v1:
time: 86.3 us; the launch traced here: 85.4 us
  local copies, waits for them, and re-layouts  26.1 us (30%)
  starting transfers between devices  24.5 us (28%)
  other arithmetic  13.9 us (16%)
  matrix products  11.3 us (13%)
  waiting for transfers between devices  8.24 us (10%)
  between operations  1.43 us (2%)
    ppermute x4, starting transfers between devices, with_halo(): after = lax.ppermute(leading, axis, down)  14.5 us
    conv_general_dilated x3, matrix products, conv_layer(): lax.conv_general_dilated(inputs, kernel, (1, 1), 'VALID', dimension_numbe...  11.3 us
    unnamed x75, local copies, waits for them, and re-layouts  7.73 us
    all_to_all x1, starting transfers between devices, on_device(): lax.all_to_all(cotangent, 'gx', split_axis=3, concat_axis=2, tiled=True)  5.86 us
    ppermute x4, waiting for transfers between devices, with_halo(): before = lax.ppermute(last, axis, up)  4.43 us
    conv_general_dilated x5, local copies, waits for them, and re-layouts, conv_layer(): lax.conv_general_dilated(inputs, kernel, (1, 1), 'VALID', dimension_numbe...  4.36 us
    slice x8, local copies, waits for them, and re-layouts, advect(): nearby[offset] = jnp.roll(middle, -offset, axis=3)  3.83 us
    all_to_all x1, starting transfers between devices, on_device(): lax.all_to_all(jnp.stack(jnp.split(block_final, lax.axis_size('gx'), axis...  3.5 us
  transfers between devices with their start and end apart: 10, of which 3 were waited for; matrix products, arithmetic and copies ran while one was open for 50% of the time, Pallas kernels for 0%

profile of v1, /device:TPU:0, one launch (start us, length us, event | category | flops | bytes accessed | tf_op | source)
XLA Modules:
  0.0 85.4 jit_solution(15190325078244359014)
XLA Ops:
  2.0 5.1 %collective-permute-start.1 = (bf16[3,4,3,128]{3,2,1,0:T(4,128)(2,1)S(1)}, bf16[3,4,3,128]{3,2,1,0:T(4,128)(2,1)S(1)}, u32[]{:S(2)}, u32[]{:S(2)}) collective-permute-start(bf16[3,4,3,128]{3,2,1,0:T(4,128)(2,1)S(1)} %get-tuple-element.171), channel_id=1, source_target_pairs={{1,0},{2,1},{3,2},{4,3},{5,4},{6,5},{7,6},{8,7},{9,8},{10,9},{11,1... | collective-permute-start | bytes 27656 | tf_op jit(solution)/shard_map/ppermute | solution.py:21
  7.1 1.5 %fusion.157 = (f32[3,8,2,128]{3,2,1,0:T(2,128)}, f32[3,8,2,128]{3,2,1,0:T(2,128)}) fusion(bf16[3,8,8,128]{3,2,1,0:T(8,128)(2,1)} %param.7), kind=kLoop, calls=%fused_computation.357 | loop fusion | bytes 98304 | tf_op jit(solution)/shard_map/slice | solution.py:19
  9.3 1.1 %copy.102 = f32[3,4,8,128]{2,1,0,3:T(4,128)S(1)} copy(f32[3,4,8,128]{3,2,1,0:T(8,128)} %param.12) | data formatting | bytes 98304 | tf_op args[5]
  10.4 1.4 %reshape.466 = f32[16,1,768]{2,1,0:T(1,128)} reshape(f32[128,3,4,8]{3,2,1,0:T(4,128)S(1)} %bitcast.528) | data formatting | bytes 98304
  11.8 5.9 %all-to-all-start.1 = ((f32[16,1,768]{2,1,0:T(1,128)}), f32[16,1,768]{2,1,0:T(1,128)}, u32[]{:S(2)}, u32[]{:S(2)}) async-start(f32[16,1,768]{2,1,0:T(1,128)} %reshape.466), calls=%async_computation.1 | async-start | bytes 98304 | tf_op jit(solution)/shard_map/all_to_all | solution.py:142
  18.5 1.5 %fusion.160 = (f32[3,4,8,1]{3,2,1,0:T(8,128)}, f32[3,4,8,1]{3,2,1,0:T(8,128)S(1)}) fusion(bf16[3,8,8,128]{3,2,1,0:T(8,128)(2,1)} %param.7), kind=kLoop, calls=%fused_computation.360 | loop fusion | bytes 1536 | tf_op jit(solution)/shard_map/jvp(jit(_roll_static))/slice | solution.py:110
  30.4 1.9 %copy.86 = bf16[9,14,32,19]{2,0,3,1:T(8,128)(2,1)S(1)} copy(bf16[9,14,32,19]{3,2,1,0:T(8,128)(2,1)S(1)} %fusion.36) | data formatting | bytes 306432 | tf_op jit(solution)/shard_map/conv_general_dilated | solution.py:71
  32.3 4.4 %select_bitcast_fusion = bf16[12,4,8,17,64]{4,2,1,3,0:T(8,128)(2,1)S(1)} fusion(pred[32,17]{0,1:T(8,128)(4,1)S(1)} %copy-done.23, bf16[9,14,32,19]{2,0,3,1:T(8,128)(2,1)S(1)} %copy.86, bf16[64,9,3,3]{0,3,2,1:T(4,128)(2,1)} %param.9), kind=kOutput, calls=%fused_computation.30 | convolution fusion | flops 72278016 | bytes 999712 | tf_op jit(solution)/shard_map/conv_general_dilated | solution.py:71
  36.9 4.0 %select_bitcast_fusion.1 = bf16[10,4,8,17,64]{4,2,1,3,0:T(8,128)(2,1)S(1)} fusion(pred[32,17]{0,1:T(8,128)(4,1)S(1)} %copy-done.22, bf16[64,64,3,3]{1,0,3,2:T(8,128)(2,1)S(1)} %copy-done, bf16[12,4,7,2,64]{4,2,1,3,0:T(8,128)(2,1)S(1)} %slice.444, bf16[12,4,8,17,64]{4,2,1,3,0:T(8,128)(2,1)S(1)} %select_bitcast_fusion), kind=kOutput, calls=%fused_computation.37 | convolution fusion | flops 407363584 | bytes 1692192 | tf_op jit(solution)/shard_map/conv_general_dilated | solution.py:71
  40.9 2.9 %fusion.28 = f32[8,32,17,36]{3,1,2,0:T(8,128)S(1)} fusion(bf16[36,64,3,3]{1,0,3,2:T(8,128)(2,1)S(1)} %copy-done.21, bf16[10,4,7,2,64]{4,2,1,3,0:T(8,128)(2,1)S(1)} %slice.445, bf16[10,4,8,17,64]{4,2,1,3,0:T(8,128)(2,1)S(1)} %select_bitcast_fusion.1), kind=kOutput, calls=%fused_computation.33 | convolution fusion | flops 182820864 | bytes 1436160 | tf_op jit(solution)/shard_map/conv_general_dilated | solution.py:71
  43.8 1.3 %copy.88 = f32[8,32,17,36]{3,0,2,1:T(8,128)S(1)} copy(f32[8,32,17,36]{3,1,2,0:T(8,128)S(1)} %fusion.28) | data formatting | bytes 1253376 | tf_op jit(solution)/shard_map/conv_general_dilated | solution.py:71
  45.2 0.9 %copy.110 = f32[8,4,128,36]{2,0,1,3:T(8,128)S(1)} copy(f32[8,4,128,36]{3,0,2,1:T(8,128)S(1)} %slice.446) | data formatting | bytes 1179648
  46.9 1.3 %broadcast_multiply_fusion.1 = (f32[4,8,128]{2,1,0:T(8,128)S(1)}, f32[4,8,128]{2,1,0:T(8,128)S(1)}, f32[4,8,128]{2,1,0:T(8,128)S(1)}, f32[4,8,128]{2,1,0:T(8,128...) fusion(f32[3,4,8,1]{3,2,1,0:T(8,128)S(1)} %get-tuple-element.173, f32[3,4,8,127]{3,2,1,0:T(8,128)S(1)} %get-tuple-element.175, ...), kind=kLoop, calls=%fused_computation.304 | loop fusion | flops 45056 | bytes 385024 | tf_op jit(solution)/shard_map/transpose(jvp())/mul | solution.py:119
  49.0 1.0 %fusion.73 = f32[3,4,8,128]{3,2,1,0:T(8,128)S(1)} fusion(f32[3,4,8,2]{3,2,1,0:T(8,128)S(1)} %copy-done.5, f32[3,4,8,126]{3,2,1,0:T(8,128)S(1)} %copy-done.7, f32[3,4,8,126]{3,2,1,0:T(8,128)S(1)} %copy-done.6, f32[3,4,8,2]{3,2,1,0:T(8,128)S(1)} %copy-done.4, f32[3,8,8,128]{3,2,1,0:T(8,128)S(1)} %convert_element_type.54, ...), kind=kLoop, calls=%fused_computation.144 | loop fusion | flops 774144 | bytes 1523712 | tf_op jit(solution)/shard_map/jvp()/sub | solution.py:120
  50.2 4.4 %collective-permute-start.4 = (f32[3,8,2,128]{3,2,1,0:T(2,128)S(1)}, f32[3,8,2,128]{3,2,1,0:T(2,128)S(1)}, u32[]{:S(2)}, u32[]{:S(2)}) collective-permute-start(f32[3,8,2,128]{3,2,1,0:T(2,128)S(1)} %get-tuple-element.111), channel_id=1, source_target_pairs={{1,0},{2,1},{3,2},{4,3},{5,4},{6,5},{7,6},{8,7},{9,8},{10,9},{11,1... | collective-permute-start | bytes 73736 | tf_op jit(solution)/shard_map/ppermute | solution.py:21
  54.7 1.4 %collective-permute-done.4 = f32[3,8,2,128]{3,2,1,0:T(2,128)S(1)} collective-permute-done((f32[3,8,2,128]{3,2,1,0:T(2,128)S(1)}, f32[3,8,2,128]{3,2,1,0:T(2,128)S(1)}, u32[]{:S(2)}, u32[]{:S(2)}) %collective-permute-start.4) | collective-permute-done | bytes 24608 | tf_op jit(solution)/shard_map/ppermute | solution.py:21
  56.2 4.4 %collective-permute-done.5 = f32[3,8,2,128]{3,2,1,0:T(2,128)S(1)} collective-permute-done((f32[3,8,2,128]{3,2,1,0:T(2,128)S(1)}, f32[3,8,2,128]{3,2,1,0:T(2,128)S(1)}, u32[]{:S(2)}, u32[]{:S(2)}) %collective-permute-start.5) | collective-permute-done | bytes 24608 | tf_op jit(solution)/shard_map/ppermute | solution.py:20
  61.2 1.5 %reduce = f32[16,768]{1,0:T(8,128)S(1)} reduce(f32[16,1,768]{2,1,0:T(1,128)} %all-to-all-done.1, f32[]{:T(128)} %broadcast.630), dimensions={1}, to_apply=%all_to_all.17.reduce_sub_computation | reduce | bytes 98308 | tf_op jit(solution)/shard_map/all_to_all | solution.py:142
  62.8 0.9 %reshape.467 = f32[128,3,4,8]{3,2,1,0:T(4,128)S(1)} reshape(f32[16,768]{1,0:T(8,128)S(1)} %reduce) | data formatting | bytes 98304
  65.8 4.4 %collective-permute-start.7 = (bf16[3,4,2,128]{3,2,1,0:T(2,128)(2,1)S(1)}, bf16[3,4,2,128]{3,2,1,0:T(2,128)(2,1)}, u32[]{:S(2)}, u32[]{:S(2)}) collective-permute-start(bf16[3,4,2,128]{3,2,1,0:T(2,128)(2,1)S(1)} %get-tuple-element.95), channel_id=1, source_target_pairs={{1,0},{2,1},{3,2},{4,3},{5,4},{6,5},{7,6},{8,7},{9,8},{10,9},{11,1... | collective-permute-start | bytes 18440 | tf_op jit(solution)/shard_map/ppermute | solution.py:21
  71.5 1.0 %reshape.464 = f32[16,1,768]{2,1,0:T(1,128)} reshape(f32[16,3,4,8,8]{4,3,2,1,0:T(8,128)S(1)} %fusion.49) | data formatting | bytes 98304
  72.6 3.5 %all-to-all-start = ((f32[16,1,768]{2,1,0:T(1,128)}), f32[16,1,768]{2,1,0:T(1,128)S(1)}, u32[]{:S(2)}, u32[]{:S(2)}) async-start(f32[16,1,768]{2,1,0:T(1,128)} %reshape.464), calls=%async_computation | async-start | bytes 98304 | tf_op jit(solution)/shard_map/all_to_all | solution.py:172
  80.5 2.4 %all-to-all-done = f32[16,1,768]{2,1,0:T(1,128)S(1)} async-done(((f32[16,1,768]{2,1,0:T(1,128)}), f32[16,1,768]{2,1,0:T(1,128)S(1)}, u32[]{:S(2)}, u32[]{:S(2)}) %all-to-all-start) | async-done | bytes 49184 | tf_op jit(solution)/shard_map/all_to_all | solution.py:172
  84.4 0.9 %reshape.445 = f32[3,4,128,8]{2,3,1,0:T(8,128)} reshape(f32[3,4,16,8,8]{3,2,4,1,0:T(8,128)S(1)} %copy.101) | data formatting | bytes 98304 | tf_op jit(solution)/shard_map/reshape | solution.py:171
  (159 shorter events, 24.8 us)
Async XLA Ops:
  0.6 36.2 %copy-start = (bf16[64,64,3,3]{1,0,3,2:T(8,128)(2,1)S(1)}, bf16[64,64,3,3]{1,0,3,2:T(8,128)(2,1)}, u32[]{:S(2)}) copy-start(bf16[64,64,3,3]{1,0,3,2:T(8,128)(2,1)} %param.10) | copy-start | bytes 221188
  0.6 27.0 %copy-start.20 = (f32[4]{0:T(128)S(1)}, f32[4]{0:T(128)}, u32[]{:S(2)}) copy-start(f32[4]{0:T(128)} %constant.69.clone) | copy-start | bytes 52
  0.7 19.4 %copy-start.1 = (bf16[3,8,8,128]{3,2,1,0:T(8,128)(2,1)S(1)}, bf16[3,8,8,128]{3,2,1,0:T(8,128)(2,1)}, u32[]{:S(2)}) copy-start(bf16[3,8,8,128]{3,2,1,0:T(8,128)(2,1)} %param.7) | copy-start | bytes 147460
  0.7 24.2 %copy-start.19 = (s32[3]{0:T(128)S(1)}, s32[3]{0:T(128)}, u32[]{:S(2)}) copy-start(s32[3]{0:T(128)} %param.8) | copy-start | bytes 40
  1.5 26.2 %collective-permute-start = (bf16[3,4,3,128]{3,2,1,0:T(4,128)(2,1)S(1)}, bf16[3,4,3,128]{3,2,1,0:T(4,128)(2,1)S(1)}, u32[]{:S(2)}, u32[]{:S(2)}) collective-permute-start(bf16[3,4,3,128]{3,2,1,0:T(4,128)(2,1)S(1)} %get-tuple-element.170), channel_id=1, source_target_pairs={{0,1},{1,2},{2,3},{3,4},{4,5},{5,6},{6,7},{7,8},{8,9},{9,10},{10,1... | collective-permute-start | bytes 27656 | tf_op jit(solution)/shard_map/ppermute | solution.py:20
  2.0 25.7 %collective-permute-start.1 = (bf16[3,4,3,128]{3,2,1,0:T(4,128)(2,1)S(1)}, bf16[3,4,3,128]{3,2,1,0:T(4,128)(2,1)S(1)}, u32[]{:S(2)}, u32[]{:S(2)}) collective-permute-start(bf16[3,4,3,128]{3,2,1,0:T(4,128)(2,1)S(1)} %get-tuple-element.171), channel_id=1, source_target_pairs={{1,0},{2,1},{3,2},{4,3},{5,4},{6,5},{7,6},{8,7},{9,8},{10,9},{11,1... | collective-permute-start | bytes 27656 | tf_op jit(solution)/shard_map/ppermute | solution.py:21
  8.6 38.3 %collective-permute-start.2 = (f32[3,8,2,128]{3,2,1,0:T(2,128)}, f32[3,8,2,128]{3,2,1,0:T(2,128)}, u32[]{:S(2)}, u32[]{:S(2)}) collective-permute-start(f32[3,8,2,128]{3,2,1,0:T(2,128)} %get-tuple-element.166), channel_id=1, source_target_pairs={{1,0},{2,1},{3,2},{4,3},{5,4},{6,5},{7,6},{8,7},{9,8},{10,9},{11,1... | collective-permute-start | bytes 73736 | tf_op jit(solution)/shard_map/ppermute | solution.py:21
  9.3 38.9 %collective-permute-start.3 = (f32[3,8,2,128]{3,2,1,0:T(2,128)}, f32[3,8,2,128]{3,2,1,0:T(2,128)}, u32[]{:S(2)}, u32[]{:S(2)}) collective-permute-start(f32[3,8,2,128]{3,2,1,0:T(2,128)} %get-tuple-element.167), channel_id=1, source_target_pairs={{0,1},{1,2},{2,3},{3,4},{4,5},{5,6},{6,7},{7,8},{8,9},{9,10},{10,1... | collective-permute-start | bytes 73736 | tf_op jit(solution)/shard_map/ppermute | solution.py:20
  11.8 48.9 %all-to-all-start.1 = ((f32[16,1,768]{2,1,0:T(1,128)}), f32[16,1,768]{2,1,0:T(1,128)}, u32[]{:S(2)}, u32[]{:S(2)}) async-start(f32[16,1,768]{2,1,0:T(1,128)} %reshape.466), calls=%async_computation.1 | async-start | bytes 98304 | tf_op jit(solution)/shard_map/all_to_all | solution.py:142
  48.9 7.2 %copy-start.16 = (f32[4,8,128]{2,1,0:T(8,128)}, f32[4,8,128]{2,1,0:T(8,128)S(1)}, u32[]{:S(2)}) copy-start(f32[4,8,128]{2,1,0:T(8,128)S(1)} %get-tuple-element.117) | copy-start | bytes 49156
  50.2 5.9 %collective-permute-start.4 = (f32[3,8,2,128]{3,2,1,0:T(2,128)S(1)}, f32[3,8,2,128]{3,2,1,0:T(2,128)S(1)}, u32[]{:S(2)}, u32[]{:S(2)}) collective-permute-start(f32[3,8,2,128]{3,2,1,0:T(2,128)S(1)} %get-tuple-element.111), channel_id=1, source_target_pairs={{1,0},{2,1},{3,2},{4,3},{5,4},{6,5},{7,6},{8,7},{9,8},{10,9},{11,1... | collective-permute-start | bytes 73736 | tf_op jit(solution)/shard_map/ppermute | solution.py:21
  54.7 6.0 %collective-permute-start.5 = (f32[3,8,2,128]{3,2,1,0:T(2,128)S(1)}, f32[3,8,2,128]{3,2,1,0:T(2,128)S(1)}, u32[]{:S(2)}, u32[]{:S(2)}) collective-permute-start(f32[3,8,2,128]{3,2,1,0:T(2,128)S(1)} %get-tuple-element.110), channel_id=1, source_target_pairs={{0,1},{1,2},{2,3},{3,4},{4,5},{5,6},{6,7},{7,8},{8,9},{9,10},{10,1... | collective-permute-start | bytes 73736 | tf_op jit(solution)/shard_map/ppermute | solution.py:20
  65.7 11.4 %copy-start.17 = (f32[4,8,128]{2,1,0:T(8,128)S(1)}, f32[4,8,128]{2,1,0:T(8,128)}, u32[]{:S(2)}) copy-start(f32[4,8,128]{2,1,0:T(8,128)} %copy-done.16) | copy-start | bytes 49156
  65.7 10.5 %collective-permute-start.6 = (bf16[3,4,2,128]{3,2,1,0:T(2,128)(2,1)S(1)}, bf16[3,4,2,128]{3,2,1,0:T(2,128)(2,1)}, u32[]{:S(2)}, u32[]{:S(2)}) collective-permute-start(bf16[3,4,2,128]{3,2,1,0:T(2,128)(2,1)S(1)} %get-tuple-element.94), channel_id=1, source_target_pairs={{0,1},{1,2},{2,3},{3,4},{4,5},{5,6},{6,7},{7,8},{8,9},{9,10},{10,1... | collective-permute-start | bytes 18440 | tf_op jit(solution)/shard_map/ppermute | solution.py:20
  65.8 10.4 %collective-permute-start.7 = (bf16[3,4,2,128]{3,2,1,0:T(2,128)(2,1)S(1)}, bf16[3,4,2,128]{3,2,1,0:T(2,128)(2,1)}, u32[]{:S(2)}, u32[]{:S(2)}) collective-permute-start(bf16[3,4,2,128]{3,2,1,0:T(2,128)(2,1)S(1)} %get-tuple-element.95), channel_id=1, source_target_pairs={{1,0},{2,1},{3,2},{4,3},{5,4},{6,5},{7,6},{8,7},{9,8},{10,9},{11,1... | collective-permute-start | bytes 18440 | tf_op jit(solution)/shard_map/ppermute | solution.py:21
  70.2 6.9 %copy-start.18 = (f32[4,8,128]{2,1,0:T(8,128)S(1)}, f32[4,8,128]{2,1,0:T(8,128)}, u32[]{:S(2)}) copy-start(f32[4,8,128]{2,1,0:T(8,128)} %get-tuple-element.114) | copy-start | bytes 49156
  70.7 6.6 %copy-start.12 = (f32[3,1,1,4,8,2]{5,4,3,0,2,1:T(8,128)S(1)}, f32[3,1,1,4,8,2]{5,4,3,0,2,1:T(8,128)}, u32[]{:S(2)}) copy-start(f32[3,1,1,4,8,2]{5,4,3,0,2,1:T(8,128)} %get-tuple-element.86) | copy-start | bytes 2308
  70.7 6.6 %copy-start.13 = (f32[3,1,1,4,8,126]{5,4,3,0,2,1:T(8,128)S(1)}, f32[3,1,1,4,8,126]{5,4,3,0,2,1:T(8,128)}, u32[]{:S(2)}) copy-start(f32[3,1,1,4,8,126]{5,4,3,0,2,1:T(8,128)} %get-tuple-element.88) | copy-start | bytes 145156
  70.7 6.6 %copy-start.14 = (f32[3,1,1,4,8,127]{5,4,3,0,2,1:T(8,128)S(1)}, f32[3,1,1,4,8,127]{5,4,3,0,2,1:T(8,128)}, u32[]{:S(2)}) copy-start(f32[3,1,1,4,8,127]{5,4,3,0,2,1:T(8,128)} %get-tuple-element.90) | copy-start | bytes 146308
  70.7 6.6 %copy-start.15 = (f32[3,1,1,4,8,1]{5,4,3,0,2,1:T(8,128)S(1)}, f32[3,1,1,4,8,1]{5,4,3,0,2,1:T(8,128)}, u32[]{:S(2)}) copy-start(f32[3,1,1,4,8,1]{5,4,3,0,2,1:T(8,128)} %get-tuple-element.92) | copy-start | bytes 1156
  71.1 6.3 %copy-start.9 = (f32[3,1,1,4,8,126]{5,4,3,0,2,1:T(8,128)S(1)}, f32[3,1,1,4,8,126]{5,4,3,0,2,1:T(8,128)}, u32[]{:S(2)}) copy-start(f32[3,1,1,4,8,126]{5,4,3,0,2,1:T(8,128)} %get-tuple-element.89) | copy-start | bytes 145156
  71.1 6.3 %copy-start.10 = (f32[3,1,1,4,8,127]{5,4,3,0,2,1:T(8,128)S(1)}, f32[3,1,1,4,8,127]{5,4,3,0,2,1:T(8,128)}, u32[]{:S(2)}) copy-start(f32[3,1,1,4,8,127]{5,4,3,0,2,1:T(8,128)} %get-tuple-element.91) | copy-start | bytes 146308
  71.1 6.3 %copy-start.11 = (f32[3,1,1,4,8,1]{5,4,3,0,2,1:T(8,128)S(1)}, f32[3,1,1,4,8,1]{5,4,3,0,2,1:T(8,128)}, u32[]{:S(2)}) copy-start(f32[3,1,1,4,8,1]{5,4,3,0,2,1:T(8,128)} %get-tuple-element.93) | copy-start | bytes 1156
  72.6 10.2 %all-to-all-start = ((f32[16,1,768]{2,1,0:T(1,128)}), f32[16,1,768]{2,1,0:T(1,128)S(1)}, u32[]{:S(2)}, u32[]{:S(2)}) async-start(f32[16,1,768]{2,1,0:T(1,128)} %reshape.464), calls=%async_computation | async-start | bytes 98304 | tf_op jit(solution)/shard_map/all_to_all | solution.py:172
  (10 other events, 32.6 us)
